TPU v7x, 256 devices: a whole 4x4x8 slice. The times are simulated.
256 devices in a mesh: seq: 32 (over z, x), tp: 8 (over y, core).
Axes of the slice: x: 4, y: 4, z: 8, core: 2. Of those that a mesh axis runs over, the one named last changes fastest.
Arguments:
- tokens_in: bfloat16 [8, 4, 2560], P(None, None, 'tp'), may hold values from -32 to 32
- attn_gain: bfloat16 [2560], replicated, may hold values from 0.25 to 1.75
- mlp_gain: bfloat16 [2560], replicated, may hold values from 0.25 to 1.75
- proj_query: bfloat16 [2560, 2560], P(None, 'tp'), may hold values from -0.125 to 0.125
- proj_key: bfloat16 [2560, 640], P(None, 'tp'), may hold values from -0.125 to 0.125
- proj_value: bfloat16 [2560, 640], P(None, 'tp'), may hold values from -0.125 to 0.125
- proj_out: bfloat16 [2560, 2560], P('tp'), may hold values from -0.125 to 0.125
- proj_gate: bfloat16 [2560, 3456], P(None, 'tp'), may hold values from -0.125 to 0.125
- proj_up: bfloat16 [2560, 3456], P(None, 'tp'), may hold values from -0.125 to 0.125
- proj_down: bfloat16 [3456, 2560], P('tp'), may hold values from -0.109375 to 0.109375
- long_keys: bfloat16 [4096, 8, 80], P('seq', 'tp'), may hold values from -340 to 340
- long_values: bfloat16 [4096, 8, 80], P('seq', 'tp'), may hold values from -6 to 6
- short_keys: bfloat16 [512, 8, 240], P('seq', 'tp'), may hold values from -340 to 340
- short_values: bfloat16 [512, 8, 240], P('seq', 'tp'), may hold values from -6 to 6
- long_seen: int32 [1], replicated, may hold values from 4096 to 8191
- short_len: int32 [3], replicated, may hold values from 1 to 504, as said below
Outputs:
- layer_out: bfloat16 [8, 4, 2560], P(None, None, 'tp')
Inputs may be any that keep to these rules, and one draw needn't show every extreme that they name: `short_len`: some short request has exactly 504 cached tokens and some exactly 1.
All inputs are finite; a program needn't handle non-finite values.
Results may differ from a plain program's by a relative error of at most 0.01.
Values may be sent and summed in bfloat16 or wider, within the bound.
No kernel may reach another device: no remote copies, remote signals or barrier semaphores. Data moves between devices by JAX's collectives and lax.ppermute only.
A program may use at most 128 MiB of HBM per device.

v0:
```python
import math
import jax
import jax.numpy as jnp
from jax import lax
from jax.sharding import PartitionSpec as P

HEADS = 32
KV_HEADS = 8
HD = 80
WIN = 4096
STEPS = 8
LONG = 1
eps_norm = 1e-05
theta_base = 10000.0
masked_score = -1e30


def rms_scaled(hidden_rows, norm_gain):
    mean_square = jnp.mean(hidden_rows * hidden_rows, axis=-1, keepdims=True)
    return hidden_rows * lax.rsqrt(mean_square + eps_norm) * norm_gain.astype(jnp.float32)


def rotate(vectors, positions):
    half_width = vectors.shape[-1] // 2
    freq_index = jnp.arange(half_width, dtype=jnp.float32)
    frequency = theta_base ** (-2.0 * freq_index / vectors.shape[-1])
    angles = positions.astype(jnp.float32)[..., None] * frequency
    view_shape = angles.shape[:2] + (1,) * (vectors.ndim - 3) + (half_width,)
    cosine_table = jnp.cos(angles).reshape(view_shape)
    sine_table = jnp.sin(angles).reshape(view_shape)
    front_part = vectors[..., :half_width]
    back_part = vectors[..., half_width:]
    return jnp.concatenate(
        [
            front_part * cosine_table - back_part * sine_table,
            back_part * cosine_table + front_part * sine_table,
        ],
        axis=-1,
    )


def partial_softmax(queries, cache_keys, cache_values, valid_mask):
    score_scale = 1.0 / math.sqrt(queries.shape[-1])
    scores = (
        jnp.einsum("trkgd,wkrd->trkgw", queries, cache_keys, preferred_element_type=jnp.float32)
        * score_scale
    )
    live_mask = valid_mask[:, :, None, None, :]
    scores = jnp.where(live_mask, scores, masked_score)
    top_score = jnp.max(scores, axis=-1)
    weights = jnp.where(live_mask, jnp.exp(scores - top_score[..., None]), 0.0)
    weight_sum = jnp.sum(weights, axis=-1)
    weighted = jnp.einsum(
        "trkgw,wkrd->trkgd",
        weights.astype(jnp.bfloat16),
        cache_values,
        preferred_element_type=jnp.float32,
    )
    return (top_score, weight_sum, weighted)


def body(
    tokens_in,
    attn_gain,
    mlp_gain,
    proj_query,
    proj_key,
    proj_value,
    proj_out,
    proj_gate,
    proj_up,
    proj_down,
    long_keys,
    long_values,
    short_keys,
    short_values,
    long_seen,
    short_len,
):
    seq_rank = lax.axis_index("seq")
    tp_rank = lax.axis_index("tp")
    local_width = tokens_in.shape[2]
    model_width = proj_query.shape[0]
    total_reqs = tokens_in.shape[1]
    group_size = HEADS // KV_HEADS
    kv_local = proj_key.shape[1] // HD
    base_pos = jnp.concatenate([long_seen, short_len])
    roll_start = long_seen % WIN
    long_slots = long_keys.shape[0]
    short_slots = short_keys.shape[0]
    long_global = seq_rank * long_slots + jnp.arange(long_slots, dtype=jnp.int32)
    long_age = (long_global[None, :] - roll_start[:, None]) % WIN
    short_global = seq_rank * short_slots + jnp.arange(short_slots, dtype=jnp.int32)
    short_live = short_global[None, :] < short_len[:, None]
    long_key_view = long_keys.reshape(long_slots, kv_local, LONG, HD)
    long_value_view = long_values.reshape(long_slots, kv_local, LONG, HD)
    short_key_view = short_keys.reshape(short_slots, kv_local, total_reqs - LONG, HD)
    short_value_view = short_values.reshape(short_slots, kv_local, total_reqs - LONG, HD)
    collected = []
    prior_keys = []
    prior_values = []
    for step_num in range(STEPS):
        token_rows = tokens_in[step_num : step_num + 1]
        block_steps = token_rows.shape[0]
        full_rows = lax.all_gather(token_rows, "tp", axis=2, tiled=True)
        normed = rms_scaled(full_rows.astype(jnp.float32), attn_gain).astype(jnp.bfloat16)
        flat_rows = normed.reshape(block_steps * total_reqs, model_width)
        steps_here = step_num + jnp.arange(block_steps, dtype=jnp.int32)
        positions = steps_here[:, None] + base_pos[None, :]
        queries = jnp.dot(flat_rows, proj_query, preferred_element_type=jnp.float32)
        queries = rotate(
            queries.reshape(block_steps, total_reqs, kv_local, group_size, HD), positions
        ).astype(jnp.bfloat16)
        key_new = jnp.dot(flat_rows, proj_key, preferred_element_type=jnp.float32)
        key_new = rotate(key_new.reshape(block_steps, total_reqs, kv_local, HD), positions).astype(
            jnp.bfloat16
        )
        value_new = jnp.dot(flat_rows, proj_value, preferred_element_type=jnp.float32)
        value_new = value_new.reshape(block_steps, total_reqs, kv_local, HD).astype(jnp.bfloat16)
        every_key = jnp.concatenate(prior_keys + [key_new], axis=0).transpose(0, 2, 1, 3)
        every_value = jnp.concatenate(prior_values + [value_new], axis=0).transpose(0, 2, 1, 3)
        token_ids = jnp.arange(every_key.shape[0], dtype=jnp.int32)
        fresh_valid = jnp.broadcast_to(
            token_ids[None, None, :] <= steps_here[:, None, None],
            (block_steps, total_reqs, every_key.shape[0]),
        )
        long_valid = long_age[None, :, :] > steps_here[:, None, None]
        short_valid = short_live[None]
        long_part = partial_softmax(queries[:, :LONG], long_key_view, long_value_view, long_valid)
        short_part = partial_softmax(
            queries[:, LONG:], short_key_view, short_value_view, short_valid
        )
        old_top = jnp.concatenate([long_part[0], short_part[0]], axis=1)
        old_sum = jnp.concatenate([long_part[1], short_part[1]], axis=1)
        old_acc = jnp.concatenate([long_part[2], short_part[2]], axis=1)
        global_top = lax.pmax(old_top, "seq")
        rescale = jnp.exp(old_top - global_top)
        old_sum, old_acc = lax.psum((old_sum * rescale, old_acc * rescale[..., None]), "seq")
        old_top = global_top
        new_top, new_sum, new_acc = partial_softmax(queries, every_key, every_value, fresh_valid)
        both_top = jnp.maximum(old_top, new_top)
        old_factor = jnp.exp(old_top - both_top)
        new_factor = jnp.exp(new_top - both_top)
        attended = (old_acc * old_factor[..., None] + new_acc * new_factor[..., None]) / (
            old_sum * old_factor + new_sum * new_factor
        )[..., None]
        attended = attended.astype(jnp.bfloat16).reshape(
            block_steps * total_reqs, kv_local * group_size * HD
        )
        head_term = jnp.dot(attended, proj_out, preferred_element_type=jnp.float32).reshape(
            block_steps, total_reqs, model_width
        )
        stream_full = full_rows.astype(jnp.float32) + lax.psum(
            head_term.astype(jnp.bfloat16), "tp"
        ).astype(jnp.float32)
        mlp_in = rms_scaled(stream_full, mlp_gain).astype(jnp.bfloat16)
        stream = lax.dynamic_slice_in_dim(
            stream_full, tp_rank * local_width, local_width, stream_full.ndim - 1
        )
        mlp_flat = mlp_in.reshape(block_steps * total_reqs, model_width)
        gate_act = jnp.dot(mlp_flat, proj_gate, preferred_element_type=jnp.float32)
        up_act = jnp.dot(mlp_flat, proj_up, preferred_element_type=jnp.float32)
        hidden_act = (jax.nn.silu(gate_act) * up_act).astype(jnp.bfloat16)
        down_term = jnp.dot(hidden_act, proj_down, preferred_element_type=jnp.float32).reshape(
            block_steps, total_reqs, model_width
        )
        result = (
            stream
            + lax.psum_scatter(
                down_term.astype(jnp.bfloat16), "tp", scatter_dimension=2, tiled=True
            ).astype(jnp.float32)
        ).astype(jnp.bfloat16)
        result, key_new, value_new = (result, key_new, value_new)
        collected.append(result)
        prior_keys = prior_keys + [key_new]
        prior_values = prior_values + [value_new]
    output = jnp.concatenate(collected, axis=0)
    return output


def solution(mesh):
    in_specs = (
        P(None, None, "tp"),
        P(),
        P(),
        P(None, "tp"),
        P(None, "tp"),
        P(None, "tp"),
        P("tp", None),
        P(None, "tp"),
        P(None, "tp"),
        P("tp", None),
        P("seq", "tp", None),
        P("seq", "tp", None),
        P("seq", "tp", None),
        P("seq", "tp", None),
        P(),
        P(),
    )
    out_specs = P(None, None, "tp")
    return jax.shard_map(body, mesh=mesh, in_specs=in_specs, out_specs=out_specs, check_vma=False)
```

profile of v0, /device:TPU:2, one launch (start us, length us, event | category | flops | bytes accessed | tf_op | source)
XLA Modules:
  0.0 888.0 jit_solution(83622997668964139)
XLA Ops:
  9.4 14.6 %all_gather.24 = bf16[1,4,2560]{1,0,2:T(2,128)(2,1)S(1)} all-gather(bf16[1,4,320]{1,0,2:T(2,128)(2,1)} %copy.291), channel_id=1, replica_groups=mesh['seq'=32,'tp'=8] {'tp'}, dimensions={2}, use_global_device_ids=true | all-gather | bytes 23040 | tf_op jit(solution)/shard_map/all_gather | solution.py:105
  26.6 14.5 %all_gather.25 = bf16[1,4,2560]{1,0,2:T(2,128)(2,1)S(1)} all-gather(bf16[1,4,320]{1,0,2:T(2,128)(2,1)} %copy.292), channel_id=1, replica_groups=mesh['seq'=32,'tp'=8] {'tp'}, dimensions={2}, use_global_device_ids=true | all-gather | bytes 23040 | tf_op jit(solution)/shard_map/all_gather | solution.py:105
  47.1 2.1 convolution_bitcast_fusion.7
  53.7 15.0 %all_gather.27 = bf16[1,4,2560]{1,0,2:T(2,128)(2,1)S(1)} all-gather(bf16[1,4,320]{1,0,2:T(2,128)(2,1)} %copy.294), channel_id=1, replica_groups=mesh['seq'=32,'tp'=8] {'tp'}, dimensions={2}, use_global_device_ids=true | all-gather | bytes 23040 | tf_op jit(solution)/shard_map/all_gather | solution.py:105
  71.9 2.7 convolution_bitcast_fusion.4
  76.1 15.0 %all_gather.26 = bf16[1,4,2560]{1,0,2:T(2,128)(2,1)S(1)} all-gather(bf16[1,4,320]{1,0,2:T(2,128)(2,1)} %copy.293), channel_id=1, replica_groups=mesh['seq'=32,'tp'=8] {'tp'}, dimensions={2}, use_global_device_ids=true | all-gather | bytes 23040 | tf_op jit(solution)/shard_map/all_gather | solution.py:105
  99.2 15.0 %all_gather.29 = bf16[1,4,2560]{1,0,2:T(2,128)(2,1)S(1)} all-gather(bf16[1,4,320]{1,0,2:T(2,128)(2,1)} %copy.296), channel_id=1, replica_groups=mesh['seq'=32,'tp'=8] {'tp'}, dimensions={2}, use_global_device_ids=true | all-gather | bytes 23040 | tf_op jit(solution)/shard_map/all_gather | solution.py:105
  115.6 2.7 convolution_bitcast_fusion.2
  119.8 15.0 %all_gather.28 = bf16[1,4,2560]{1,0,2:T(2,128)(2,1)S(1)} all-gather(bf16[1,4,320]{1,0,2:T(2,128)(2,1)} %copy.295), channel_id=1, replica_groups=mesh['seq'=32,'tp'=8] {'tp'}, dimensions={2}, use_global_device_ids=true | all-gather | bytes 23040 | tf_op jit(solution)/shard_map/all_gather | solution.py:105
  144.6 15.0 %all_gather.31 = bf16[1,4,2560]{1,0,2:T(2,128)(2,1)S(1)} all-gather(bf16[1,4,320]{1,0,2:T(2,128)(2,1)} %copy.298), channel_id=1, replica_groups=mesh['seq'=32,'tp'=8] {'tp'}, dimensions={2}, use_global_device_ids=true | all-gather | bytes 23040 | tf_op jit(solution)/shard_map/all_gather | solution.py:105
  161.0 2.7 convolution_bitcast_fusion
  165.2 15.3 %all_gather.30 = bf16[1,4,2560]{1,0,2:T(2,128)(2,1)S(1)} all-gather(bf16[1,4,320]{1,0,2:T(2,128)(2,1)} %copy.297), channel_id=1, replica_groups=mesh['seq'=32,'tp'=8] {'tp'}, dimensions={2}, use_global_device_ids=true | all-gather | bytes 23040 | tf_op jit(solution)/shard_map/all_gather | solution.py:105
  183.3 2.1 convolution_bitcast_fusion.1
  204.0 140.7 %all-reduce.1 = (f32[1,4,1,4]{3,1,2,0:T(4,128)S(1)}, f32[1,4,1,4]{3,1,2,0:T(4,128)S(1)}, f32[1,4,1,4]{3,1,2,0:T(4,128)S(1)}, f32[1,4,1,4]{3,1,2,0:T(4,128)S(1)},...) all-reduce(f32[1,4,1,4]{3,1,2,0:T(4,128)S(1)} %pad_maximum_fusion.1, ...), channel_id=1, replica_groups=mesh['seq'=32,'tp'=8] {'seq'}, use_global_device_ids=true, to_apply=%region_3.4 | all-reduce | flops 128 | bytes 1024 | tf_op jit(solution)/shard_map/pmax | solution.py:136
  345.4 140.2 %all-reduce = (f32[1,4,1,4,80]{4,3,1,0,2:T(4,128)S(1)}, f32[1,4,1,4]{3,1,2,0:T(4,128)S(1)}, f32[1,4,1,4,80]{4,3,1,0,2:T(4,128)S(1)}, f32[1,4,1,4]{3,1,2,0:T(4,12...) all-reduce(f32[1,4,1,4,80]{4,3,1,0,2:T(4,128)S(1)} %maximum_multipl, ...), channel_id=1, replica_groups=mesh['seq'=32,'tp'=8] {'seq'}, use_global_device_ids=true, to_apply=%region_4.5 | all-reduce | flops 10368 | bytes 82944 | tf_op jit(solution)/shard_map/psum | solution.py:138
  489.1 2.4 fusion
  491.5 2.4 fusion.2
  495.1 2.4 fusion.4
  498.6 2.4 fusion.6
  502.3 2.4 fusion.8
  506.0 2.4 fusion.10
  509.4 2.4 fusion.12
  512.9 2.4 fusion.14
  515.4 62.3 %all-reduce.5.cloned.1.call-done = (bf16[1,4,2560]{2,1,0:T(4,128)(2,1)}, bf16[1,4,2560]{2,1,0:T(4,128)(2,1)}, bf16[1,4,2560]{2,1,0:T(4,128)(2,1)}, bf16[1,4,2560...) async-done(((bf16[1,4,2560]{2,1,0:T(4,128)(2,1)}, ...) | async-done | bytes 163856 | tf_op jit(solution)/shard_map/psum | solution.py:153
  579.2 2.3 fusion.633
  581.5 3.5 fusion.1
  585.1 2.1 copy.259
  589.9 2.3 fusion.629
  592.3 3.5 fusion.3
  596.5 2.3 fusion.625
  598.8 3.6 fusion.5
  603.2 2.3 fusion.621
  605.5 3.6 fusion.7
  609.8 2.3 fusion.617
  612.1 3.5 fusion.9
  616.4 2.3 fusion.613
  618.7 3.6 fusion.11
  626.7 2.9 fusion.609
  632.8 3.5 fusion.13
  636.3 2.1 copy.265
  648.8 3.0 fusion.605
  654.9 3.5 fusion.15
  663.5 32.1 %reduce-scatter.29.cloned.1.call-done = bf16[320,4]{1,0:T(8,128)(2,1)} async-done(((bf16[2560,4]{1,0:T(8,128)(2,1)}), bf16[320,4]{1,0:T(8,128)(2,1)}) %reduce-scatter.29.cloned.1.call-update) | async-done | bytes 2576
  696.6 34.4 %reduce-scatter.31.cloned.1.call-done = bf16[320,4]{1,0:T(8,128)(2,1)} async-done(((bf16[2560,4]{1,0:T(8,128)(2,1)}), bf16[320,4]{1,0:T(8,128)(2,1)}) %reduce-scatter.31.cloned.1.call-update) | async-done | bytes 2576
  732.0 34.4 %reduce-scatter.33.cloned.1.call-done = bf16[320,4]{1,0:T(8,128)(2,1)} async-done(((bf16[2560,4]{1,0:T(8,128)(2,1)}), bf16[320,4]{1,0:T(8,128)(2,1)}) %reduce-scatter.33.cloned.1.call-update) | async-done | bytes 2576
  767.4 34.6 %reduce-scatter.35.cloned.1.call-done = bf16[320,4]{1,0:T(8,128)(2,1)} async-done(((bf16[2560,4]{1,0:T(8,128)(2,1)}), bf16[320,4]{1,0:T(8,128)(2,1)}) %reduce-scatter.35.cloned.1.call-update) | async-done | bytes 2576
  802.9 34.6 %reduce-scatter.37.cloned.1.call-done = bf16[320,4]{1,0:T(8,128)(2,1)} async-done(((bf16[2560,4]{1,0:T(8,128)(2,1)}), bf16[320,4]{1,0:T(8,128)(2,1)}) %reduce-scatter.37.cloned.1.call-update) | async-done | bytes 2576
  839.2 33.8 %reduce-scatter.39.cloned.1.call-done = bf16[320,4]{1,0:T(8,128)(2,1)} async-done(((bf16[2560,4]{1,0:T(8,128)(2,1)}), bf16[320,4]{1,0:T(8,128)(2,1)}) %reduce-scatter.39.cloned.1.call-update) | async-done | bytes 2576
  (506 shorter events, 122.7 us)
Async XLA Ops:
  6.5 575.0 %copy-start = (bf16[432,2560]{1,0:T(8,128)(2,1)S(1)}, bf16[432,2560]{1,0:T(8,128)(2,1)}, u32[]{:S(2)}) copy-start(bf16[432,2560]{1,0:T(8,128)(2,1)} %param.25) | copy-start | bytes 6635524
  6.5 571.1 %all-reduce.5.cloned.1.call-start = ((), (), s32[]{:S(2)}) async-start(), calls=%async_computation.16 | async-start | bytes 327680 | tf_op jit(solution)/shard_map/psum | solution.py:153
  41.8 27.0 %copy-start.2 = (bf16[1,4,2560]{2,1,0:T(4,128)(2,1)}, bf16[1,4,2560]{2,1,0:T(4,128)(2,1)S(1)}, u32[]{:S(2)}) copy-start(bf16[1,4,2560]{2,1,0:T(4,128)(2,1)S(1)} %copy.174) | copy-start | bytes 61444
  41.8 11.1 %copy-start.52 = (bf16[1,4,320]{2,1,0:T(4,128)(2,1)S(1)}, bf16[1,4,320]{2,1,0:T(4,128)(2,1)}, u32[]{:S(2)}) copy-start(bf16[1,4,320]{2,1,0:T(4,128)(2,1)} %get-tuple-element.79) | copy-start | bytes 7684
  44.0 8.8 copy-start.62
  44.1 8.8 copy-start.58
  44.1 8.8 copy-start.60
  44.1 8.8 copy-start.64
  44.1 8.8 copy-start.66
  44.1 8.8 copy-start.68
  114.9 21.6 %copy-start.11 = (bf16[1,4,2560]{2,1,0:T(4,128)(2,1)}, bf16[1,4,2560]{2,1,0:T(4,128)(2,1)S(1)}, u32[]{:S(2)}) copy-start(bf16[1,4,2560]{2,1,0:T(4,128)(2,1)S(1)} %copy.223) | copy-start | bytes 61444
  165.2 21.5 %copy-start.1 = (bf16[128,1,80]{0,2,1:T(8,128)(2,1)S(1)}, bf16[128,1,80]{0,2,1:T(8,128)(2,1)}, u32[]{:S(2)}) copy-start(bf16[128,1,80]{0,2,1:T(8,128)(2,1)} %param.26) | copy-start | bytes 61444
  182.2 12.5 %copy-start.75 = (bf16[1,1,1,4,80]{4,1,3,2,0:T(2,128)(2,1)S(1)}, bf16[1,1,1,4,80]{4,1,3,2,0:T(2,128)(2,1)}, u32[]{:S(2)}) copy-start(bf16[1,1,1,4,80]{4,1,3,2,0:T(2,128)(2,1)} %fusion.448) | copy-start | bytes 1924
  182.2 12.8 %copy-start.100 = (bf16[128,1,80]{0,2,1:T(8,128)(2,1)S(1)}, bf16[128,1,80]{0,2,1:T(8,128)(2,1)}, u32[]{:S(2)}) copy-start(bf16[128,1,80]{0,2,1:T(8,128)(2,1)} %param.27) | copy-start | bytes 61444
  182.2 13.2 %copy-start.74 = (bf16[1,1,1,4,80]{4,1,3,2,0:T(2,128)(2,1)S(1)}, bf16[1,1,1,4,80]{4,1,3,2,0:T(2,128)(2,1)}, u32[]{:S(2)}) copy-start(bf16[1,1,1,4,80]{4,1,3,2,0:T(2,128)(2,1)} %fusion.447) | copy-start | bytes 1924
  182.2 14.4 %copy-start.55 = (bf16[16,1,240]{2,0,1:T(8,128)(2,1)S(1)}, bf16[16,1,240]{2,0,1:T(8,128)(2,1)}, u32[]{:S(2)}) copy-start(bf16[16,1,240]{2,0,1:T(8,128)(2,1)} %param.29) | copy-start | bytes 23044
  182.3 14.5 %copy-start.56 = (bf16[16,1,240]{2,0,1:T(8,128)(2,1)S(1)}, bf16[16,1,240]{2,0,1:T(8,128)(2,1)}, u32[]{:S(2)}) copy-start(bf16[16,1,240]{2,0,1:T(8,128)(2,1)} %param.28) | copy-start | bytes 23044
  182.3 14.6 %copy-start.96 = (s32[3]{0:T(128)S(1)}, s32[3]{0:T(128)}, u32[]{:S(2)}) copy-start(s32[3]{0:T(128)} %param.31) | copy-start | bytes 40
  182.3 14.7 %copy-start.76 = (bf16[3,4,80]{2,0,1:T(4,128)(2,1)S(1)}, bf16[3,4,80]{2,0,1:T(4,128)(2,1)}, u32[]{:S(2)}) copy-start(bf16[3,4,80]{2,0,1:T(4,128)(2,1)} %fusion.260) | copy-start | bytes 5764
  182.3 15.1 %copy-start.77 = (bf16[3,4,80]{2,0,1:T(4,128)(2,1)S(1)}, bf16[3,4,80]{2,0,1:T(4,128)(2,1)}, u32[]{:S(2)}) copy-start(bf16[3,4,80]{2,0,1:T(4,128)(2,1)} %fusion.259) | copy-start | bytes 5764
  182.3 15.3 %copy-start.79 = (bf16[3,4,80]{2,0,1:T(4,128)(2,1)S(1)}, bf16[3,4,80]{2,0,1:T(4,128)(2,1)}, u32[]{:S(2)}) copy-start(bf16[3,4,80]{2,0,1:T(4,128)(2,1)} %fusion.258) | copy-start | bytes 5764
  182.3 15.5 %copy-start.78 = (bf16[3,4,80]{2,0,1:T(4,128)(2,1)S(1)}, bf16[3,4,80]{2,0,1:T(4,128)(2,1)}, u32[]{:S(2)}) copy-start(bf16[3,4,80]{2,0,1:T(4,128)(2,1)} %fusion.257) | copy-start | bytes 5764
  182.3 15.7 %copy-start.81 = (bf16[3,4,80]{2,0,1:T(4,128)(2,1)S(1)}, bf16[3,4,80]{2,0,1:T(4,128)(2,1)}, u32[]{:S(2)}) copy-start(bf16[3,4,80]{2,0,1:T(4,128)(2,1)} %fusion.256) | copy-start | bytes 5764
  182.3 15.9 %copy-start.80 = (bf16[3,4,80]{2,0,1:T(4,128)(2,1)S(1)}, bf16[3,4,80]{2,0,1:T(4,128)(2,1)}, u32[]{:S(2)}) copy-start(bf16[3,4,80]{2,0,1:T(4,128)(2,1)} %fusion.255) | copy-start | bytes 5764
  182.3 18.7 %copy-start.3 = (bf16[1,4,2560]{2,1,0:T(4,128)(2,1)S(1)}, bf16[1,4,2560]{2,1,0:T(4,128)(2,1)}, u32[]{:S(2)}) copy-start(bf16[1,4,2560]{2,1,0:T(4,128)(2,1)} %copy-done.2) | copy-start | bytes 61444
  182.3 18.7 %copy-start.91 = (f32[4]{0:T(128)S(1)}, f32[4]{0:T(128)}, u32[]{:S(2)}) copy-start(f32[4]{0:T(128)} %copy-done.90) | copy-start | bytes 52
  182.4 18.7 %copy-start.98 = (bf16[2560,80]{0,1:T(8,128)(2,1)S(1)}, bf16[2560,80]{0,1:T(8,128)(2,1)}, u32[]{:S(2)}) copy-start(bf16[2560,80]{0,1:T(8,128)(2,1)} %param.20) | copy-start | bytes 1228804
  182.4 19.0 %copy-start.8 = (bf16[1,4,2560]{2,1,0:T(4,128)(2,1)S(1)}, bf16[1,4,2560]{2,1,0:T(4,128)(2,1)}, u32[]{:S(2)}) copy-start(bf16[1,4,2560]{2,1,0:T(4,128)(2,1)} %copy.166) | copy-start | bytes 61444
  182.4 19.0 %copy-start.95 = (f32[4]{0:T(128)S(1)}, f32[4]{0:T(128)}, u32[]{:S(2)}) copy-start(f32[4]{0:T(128)} %copy-done.94) | copy-start | bytes 52
  183.3 18.3 %copy-start.19 = (bf16[1,4,2560]{2,1,0:T(4,128)(2,1)S(1)}, bf16[1,4,2560]{2,1,0:T(4,128)(2,1)}, u32[]{:S(2)}) copy-start(bf16[1,4,2560]{2,1,0:T(4,128)(2,1)} %copy.212) | copy-start | bytes 61444
  183.3 18.3 %copy-start.87 = (f32[4]{0:T(128)S(1)}, f32[4]{0:T(128)}, u32[]{:S(2)}) copy-start(f32[4]{0:T(128)} %copy-done.86) | copy-start | bytes 52
  183.3 18.6 %copy-start.9 = (bf16[1,4,2560]{2,1,0:T(4,128)(2,1)S(1)}, bf16[1,4,2560]{2,1,0:T(4,128)(2,1)}, u32[]{:S(2)}) copy-start(bf16[1,4,2560]{2,1,0:T(4,128)(2,1)} %copy.200) | copy-start | bytes 61444
  183.3 18.6 %copy-start.89 = (f32[4]{0:T(128)S(1)}, f32[4]{0:T(128)}, u32[]{:S(2)}) copy-start(f32[4]{0:T(128)} %copy-done.88) | copy-start | bytes 52
  185.5 16.7 %copy-start.15 = (bf16[1,4,2560]{2,1,0:T(4,128)(2,1)S(1)}, bf16[1,4,2560]{2,1,0:T(4,128)(2,1)}, u32[]{:S(2)}) copy-start(bf16[1,4,2560]{2,1,0:T(4,128)(2,1)} %copy-done.14) | copy-start | bytes 61444
  185.5 16.7 %copy-start.93 = (f32[4]{0:T(128)S(1)}, f32[4]{0:T(128)}, u32[]{:S(2)}) copy-start(f32[4]{0:T(128)} %copy-done.92) | copy-start | bytes 52
  185.5 17.0 %copy-start.6 = (bf16[1,4,2560]{2,1,0:T(4,128)(2,1)S(1)}, bf16[1,4,2560]{2,1,0:T(4,128)(2,1)}, u32[]{:S(2)}) copy-start(bf16[1,4,2560]{2,1,0:T(4,128)(2,1)} %copy-done.5) | copy-start | bytes 61444
  185.5 17.0 %copy-start.83 = (f32[4]{0:T(128)S(1)}, f32[4]{0:T(128)}, u32[]{:S(2)}) copy-start(f32[4]{0:T(128)} %copy-done.82) | copy-start | bytes 52
  187.8 15.0 %copy-start.17 = (bf16[1,4,2560]{2,1,0:T(4,128)(2,1)S(1)}, bf16[1,4,2560]{2,1,0:T(4,128)(2,1)}, u32[]{:S(2)}) copy-start(bf16[1,4,2560]{2,1,0:T(4,128)(2,1)} %copy.234) | copy-start | bytes 61444
  201.3 285.8 %copy-start.41 = (bf16[1,4,1,4,40]{4,1,3,2,0:T(4,128)(2,1)S(1)}, bf16[1,4,1,4,40]{4,1,3,2,0:T(4,128)(2,1)}, u32[]{:S(2)}) copy-start(bf16[1,4,1,4,40]{4,1,3,2,0:T(4,128)(2,1)} %copy-done.40) | copy-start | bytes 3844
  201.4 285.7 %copy-start.43 = (bf16[1,4,1,4,40]{4,1,3,2,0:T(4,128)(2,1)S(1)}, bf16[1,4,1,4,40]{4,1,3,2,0:T(4,128)(2,1)}, u32[]{:S(2)}) copy-start(bf16[1,4,1,4,40]{4,1,3,2,0:T(4,128)(2,1)} %copy-done.42) | copy-start | bytes 3844
  515.3 146.2 %reduce-scatter.25.cloned.1.call-start = ((), (), s32[]{:S(2)}) async-start(), calls=%async_computation.8 | async-start | bytes 737280
  588.2 74.4 %reduce-scatter.27.cloned.1.call-start = ((), (), s32[]{:S(2)}) async-start(), calls=%async_computation.9 | async-start | bytes 737280
  626.6 69.0 %reduce-scatter.29.cloned.1.call-start = ((), (), s32[]{:S(2)}) async-start(), calls=%async_computation.10 | async-start | bytes 737280
  632.7 98.3 %reduce-scatter.31.cloned.1.call-start = ((), (), s32[]{:S(2)}) async-start(), calls=%async_computation.11 | async-start | bytes 737280
  639.4 127.0 %reduce-scatter.33.cloned.1.call-start = ((), (), s32[]{:S(2)}) async-start(), calls=%async_computation.12 | async-start | bytes 737280
  644.5 157.4 %reduce-scatter.35.cloned.1.call-start = ((), (), s32[]{:S(2)}) async-start(), calls=%async_computation.13 | async-start | bytes 737280
  648.7 188.7 %reduce-scatter.37.cloned.1.call-start = ((), (), s32[]{:S(2)}) async-start(), calls=%async_computation.14 | async-start | bytes 737280
  654.8 218.2 %reduce-scatter.39.cloned.1.call-start = ((), (), s32[]{:S(2)}) async-start(), calls=%async_computation.15 | async-start | bytes 737280
  (62 other events, 286.9 us)
Sparse Core Ops, SparseCore 0:
  515.4 62.2 all-reduce.4
  588.3 33.4 reduce-scatter.24
  626.7 33.4 reduce-scatter.26
  662.6 32.9 reduce-scatter.28
  698.0 32.9 reduce-scatter.30
  733.4 32.9 reduce-scatter.32
  768.9 32.9 reduce-scatter.34
  804.5 32.9 reduce-scatter.36
  840.0 32.9 reduce-scatter.38
where the time goes:
time: 892 us; the launch traced here: 888 us
  blocking collectives  400 us (45%)
  waiting for transfers between devices  266 us (30%)
  matrix products  107 us (12%)
  local copies, waits for them, and re-layouts  57.8 us (6%)
  other arithmetic  41 us (5%)
  between operations  15.4 us (2%)
    unnamed x17, waiting for transfers between devices  204 us
    pmax x1, blocking collectives, body(): global_top = lax.pmax(old_top, 'seq')  141 us
    psum x1, blocking collectives, body(): lax.psum((old_sum * rescale, old_acc * rescale[..., None]), 'seq')  140 us
    all_gather x8, blocking collectives, body(): full_rows = lax.all_gather(token_rows, 'tp', axis=2, tiled=True)  120 us
    psum x1, waiting for transfers between devices, body(): lax.psum(head_term.astype(jnp.bfloat16), 'tp').astype(jnp.float32)  62.3 us
    unnamed x247, local copies, waits for them, and re-layouts  45.7 us
    dot_general x8, matrix products, body(): jnp.dot(hidden_act, proj_down, preferred_element_type=jnp.float32)  28.3 us
    dot_general x8, matrix products, body(): gate_act = jnp.dot(mlp_flat, proj_gate, preferred_element_type=jnp.float32)  19.7 us
  transfers between devices with their start and end apart: 9, of which 7 were waited for; matrix products, arithmetic and copies ran while one was open for 9% of the time, Pallas kernels for 0%

commit v1 on v0

--- a/solution.py
+++ b/solution.py
@@ -3,6 +3,7 @@
 import jax.numpy as jnp
 from jax import lax
 from jax.sharding import PartitionSpec as P
+from jax.lax import all_gather
 
 HEADS = 32
 KV_HEADS = 8
@@ -150,7 +151,13 @@
         head_term = jnp.dot(attended, proj_out, preferred_element_type=jnp.float32).reshape(
             block_steps, total_reqs, model_width
         )
-        stream_full = full_rows.astype(jnp.float32) + lax.psum(
+
+        def view_the_sides(inp, named_axis):
+            big = all_gather(inp, named_axis)
+            w2 = jnp.sum(big, axis=0)
+            return w2
+
+        stream_full = full_rows.astype(jnp.float32) + view_the_sides(
             head_term.astype(jnp.bfloat16), "tp"
         ).astype(jnp.float32)
         mlp_in = rms_scaled(stream_full, mlp_gain).astype(jnp.bfloat16)

time: 892 us -> 811 us (0.909)
  waiting for transfers between devices: 266 us -> 51.1 us
  blocking collectives: 400 us -> 504 us
  matrix products: 107 us -> 122 us
  other arithmetic: 41 us -> 54.4 us
    unnamed x17 -> x16, waiting for transfers between devices: 204 us -> 51.1 us
    all_gather x0 -> x8, blocking collectives: none -> 103 us  [view_the_sides(): big = all_gather(inp, named_axis)]
    psum x1 -> x0, waiting for transfers between devices: 62.3 us -> none  [body(): lax.psum(head_term.astype(jnp.bfloat16), 'tp').astype(jnp.float32)]
    dot_general x8, matrix products: 4.09 us -> 14.1 us  [body(): jnp.dot(flat_rows, proj_value, preferred_element_type=jnp.float32)]
    unnamed x247 -> x265, local copies, waits for them, and re-layouts: 45.7 us -> 47 us
  transfers between devices with their start and end apart: 9 -> 8, of which waited for: 7 -> 2; matrix products, arithmetic and copies ran while one was open for 9% -> 17% of each run, Pallas kernels for 0% -> 0%
where the time goes in v1:
time: 811 us; the launch traced here: 807 us
  blocking collectives  504 us (62%)
  matrix products  122 us (15%)
  local copies, waits for them, and re-layouts  59 us (7%)
  other arithmetic  54.4 us (7%)
  waiting for transfers between devices  51.1 us (6%)
  between operations  15.7 us (2%)
    pmax x1, blocking collectives, body(): global_top = lax.pmax(old_top, 'seq')  141 us
    psum x1, blocking collectives, body(): lax.psum((old_sum * rescale, old_acc * rescale[..., None]), 'seq')  141 us
    all_gather x8, blocking collectives, body(): full_rows = lax.all_gather(token_rows, 'tp', axis=2, tiled=True)  119 us
    all_gather x8, blocking collectives, view_the_sides(): big = all_gather(inp, named_axis)  103 us
    unnamed x16, waiting for transfers between devices  51.1 us
    unnamed x265, local copies, waits for them, and re-layouts  47 us
    dot_general x8, matrix products, body(): jnp.dot(hidden_act, proj_down, preferred_element_type=jnp.float32)  27.8 us
    dot_general x8, matrix products, body(): queries = jnp.dot(flat_rows, proj_query, preferred_element_type=jnp.float32)  18.7 us
  transfers between devices with their start and end apart: 8, of which 2 were waited for; matrix products, arithmetic and copies ran while one was open for 17% of the time, Pallas kernels for 0%

profile of v1, /device:TPU:2, one launch (start us, length us, event | category | flops | bytes accessed | tf_op | source)
XLA Modules:
  0.0 806.8 jit_solution(13618688698330139441)
XLA Ops:
  9.4 14.6 %all_gather.72 = bf16[1,4,2560]{1,0,2:T(2,128)(2,1)S(1)} all-gather(bf16[1,4,320]{1,0,2:T(2,128)(2,1)} %copy.596), channel_id=1, replica_groups=mesh['seq'=32,'tp'=8] {'tp'}, dimensions={2}, use_global_device_ids=true | all-gather | bytes 23040 | tf_op jit(solution)/shard_map/all_gather | solution.py:106
  26.6 14.5 %all_gather.75 = bf16[1,4,2560]{1,0,2:T(2,128)(2,1)S(1)} all-gather(bf16[1,4,320]{1,0,2:T(2,128)(2,1)} %copy.597), channel_id=1, replica_groups=mesh['seq'=32,'tp'=8] {'tp'}, dimensions={2}, use_global_device_ids=true | all-gather | bytes 23040 | tf_op jit(solution)/shard_map/all_gather | solution.py:106
  47.1 2.1 convolution_bitcast_fusion.7
  53.8 15.0 %all_gather.81 = bf16[1,4,2560]{1,0,2:T(2,128)(2,1)S(1)} all-gather(bf16[1,4,320]{1,0,2:T(2,128)(2,1)} %copy.599), channel_id=1, replica_groups=mesh['seq'=32,'tp'=8] {'tp'}, dimensions={2}, use_global_device_ids=true | all-gather | bytes 23040 | tf_op jit(solution)/shard_map/all_gather | solution.py:106
  70.2 2.7 convolution_bitcast_fusion.4
  74.4 15.0 %all_gather.78 = bf16[1,4,2560]{1,0,2:T(2,128)(2,1)S(1)} all-gather(bf16[1,4,320]{1,0,2:T(2,128)(2,1)} %copy.598), channel_id=1, replica_groups=mesh['seq'=32,'tp'=8] {'tp'}, dimensions={2}, use_global_device_ids=true | all-gather | bytes 23040 | tf_op jit(solution)/shard_map/all_gather | solution.py:106
  99.2 15.0 %all_gather.87 = bf16[1,4,2560]{1,0,2:T(2,128)(2,1)S(1)} all-gather(bf16[1,4,320]{1,0,2:T(2,128)(2,1)} %copy.601), channel_id=1, replica_groups=mesh['seq'=32,'tp'=8] {'tp'}, dimensions={2}, use_global_device_ids=true | all-gather | bytes 23040 | tf_op jit(solution)/shard_map/all_gather | solution.py:106
  115.6 2.7 convolution_bitcast_fusion.2
  119.8 15.0 %all_gather.84 = bf16[1,4,2560]{1,0,2:T(2,128)(2,1)S(1)} all-gather(bf16[1,4,320]{1,0,2:T(2,128)(2,1)} %copy.600), channel_id=1, replica_groups=mesh['seq'=32,'tp'=8] {'tp'}, dimensions={2}, use_global_device_ids=true | all-gather | bytes 23040 | tf_op jit(solution)/shard_map/all_gather | solution.py:106
  144.6 15.0 %all_gather.93 = bf16[1,4,2560]{1,0,2:T(2,128)(2,1)S(1)} all-gather(bf16[1,4,320]{1,0,2:T(2,128)(2,1)} %copy.603), channel_id=1, replica_groups=mesh['seq'=32,'tp'=8] {'tp'}, dimensions={2}, use_global_device_ids=true | all-gather | bytes 23040 | tf_op jit(solution)/shard_map/all_gather | solution.py:106
  161.1 2.7 convolution_bitcast_fusion
  165.3 15.1 %all_gather.90 = bf16[1,4,2560]{1,0,2:T(2,128)(2,1)S(1)} all-gather(bf16[1,4,320]{1,0,2:T(2,128)(2,1)} %copy.602), channel_id=1, replica_groups=mesh['seq'=32,'tp'=8] {'tp'}, dimensions={2}, use_global_device_ids=true | all-gather | bytes 23040 | tf_op jit(solution)/shard_map/all_gather | solution.py:106
  183.3 2.2 convolution_bitcast_fusion.1
  202.8 140.9 %all-reduce.1 = (f32[1,4,1,4]{3,1,2,0:T(4,128)S(1)}, f32[1,4,1,4]{3,1,2,0:T(4,128)S(1)}, f32[1,4,1,4]{3,1,2,0:T(4,128)S(1)}, f32[1,4,1,4]{3,1,2,0:T(4,128)S(1)},...) all-reduce(f32[1,4,1,4]{3,1,2,0:T(4,128)S(1)} %pad_maximum_fusion.1, ...), channel_id=1, replica_groups=mesh['seq'=32,'tp'=8] {'seq'}, use_global_device_ids=true, to_apply=%region_3.4 | all-reduce | flops 128 | bytes 1024 | tf_op jit(solution)/shard_map/pmax | solution.py:137
  344.6 140.8 %all-reduce = (f32[1,4,1,4,80]{4,3,1,0,2:T(4,128)S(1)}, f32[1,4,1,4]{3,1,2,0:T(4,128)S(1)}, f32[1,4,1,4,80]{4,3,1,0,2:T(4,128)}, f32[1,4,1,4]{3,1,2,0:T(4,128)},...) all-reduce(f32[1,4,1,4,80]{4,3,1,0,2:T(4,128)S(1)} %maximum_multipl, ...), channel_id=1, replica_groups=mesh['seq'=32,'tp'=8] {'seq'}, use_global_device_ids=true, to_apply=%region_4.5 | all-reduce | flops 10368 | bytes 82944 | tf_op jit(solution)/shard_map/psum | solution.py:139
  488.3 13.0 %all-gather.8 = bf16[8,4,2560]{2,1,0:T(4,128)(2,1)S(1)} all-gather(bf16[1,4,2560]{2,1,0:T(4,128)(2,1)S(1)} %fusion), channel_id=2, replica_groups=mesh['seq'=32,'tp'=8] {'tp'}, dimensions={0}, use_global_device_ids=true | all-gather | bytes 184320 | tf_op jit(solution)/shard_map/all_gather | solution.py:156
  502.2 2.3 fusion.633
  504.5 3.5 fusion.1
  508.0 2.1 copy.564
  519.6 13.1 %all-gather.9 = bf16[8,4,2560]{2,1,0:T(4,128)(2,1)S(1)} all-gather(bf16[1,4,2560]{2,1,0:T(4,128)(2,1)S(1)} %fusion.2), channel_id=3, replica_groups=mesh['seq'=32,'tp'=8] {'tp'}, dimensions={0}, use_global_device_ids=true | all-gather | bytes 184320 | tf_op jit(solution)/shard_map/all_gather | solution.py:156
  533.5 2.3 fusion.629
  535.8 3.6 fusion.3
  539.4 2.1 copy.566
  553.8 12.8 %all-gather.10 = bf16[8,4,2560]{2,1,0:T(4,128)(2,1)S(1)} all-gather(bf16[1,4,2560]{2,1,0:T(4,128)(2,1)S(1)} %fusion.4), channel_id=4, replica_groups=mesh['seq'=32,'tp'=8] {'tp'}, dimensions={0}, use_global_device_ids=true | all-gather | bytes 184320 | tf_op jit(solution)/shard_map/all_gather | solution.py:156
  567.4 2.3 fusion.625
  569.7 3.5 fusion.5
  573.3 2.1 copy.568
  583.6 12.8 %all-gather.11 = bf16[8,4,2560]{2,1,0:T(4,128)(2,1)S(1)} all-gather(bf16[1,4,2560]{2,1,0:T(4,128)(2,1)S(1)} %fusion.6), channel_id=5, replica_groups=mesh['seq'=32,'tp'=8] {'tp'}, dimensions={0}, use_global_device_ids=true | all-gather | bytes 184320 | tf_op jit(solution)/shard_map/all_gather | solution.py:156
  597.2 2.3 fusion.621
  599.5 3.5 fusion.7
  603.1 2.1 copy.570
  615.9 13.0 %all-gather.12 = bf16[8,4,2560]{2,1,0:T(4,128)(2,1)S(1)} all-gather(bf16[1,4,2560]{2,1,0:T(4,128)(2,1)S(1)} %fusion.8), channel_id=6, replica_groups=mesh['seq'=32,'tp'=8] {'tp'}, dimensions={0}, use_global_device_ids=true | all-gather | bytes 184320 | tf_op jit(solution)/shard_map/all_gather | solution.py:156
  629.7 2.3 fusion.617
  632.0 3.6 fusion.9
  635.6 2.1 copy.572
  651.2 12.8 %all-gather.13 = bf16[8,4,2560]{2,1,0:T(4,128)(2,1)S(1)} all-gather(bf16[1,4,2560]{2,1,0:T(4,128)(2,1)S(1)} %fusion.10), channel_id=7, replica_groups=mesh['seq'=32,'tp'=8] {'tp'}, dimensions={0}, use_global_device_ids=true | all-gather | bytes 184320 | tf_op jit(solution)/shard_map/all_gather | solution.py:156
  664.8 2.3 fusion.613
  667.1 3.6 fusion.11
  670.6 2.1 copy.574
  681.6 12.8 %all-gather.14 = bf16[8,4,2560]{2,1,0:T(4,128)(2,1)S(1)} all-gather(bf16[1,4,2560]{2,1,0:T(4,128)(2,1)S(1)} %fusion.12), channel_id=8, replica_groups=mesh['seq'=32,'tp'=8] {'tp'}, dimensions={0}, use_global_device_ids=true | all-gather | bytes 184320 | tf_op jit(solution)/shard_map/all_gather | solution.py:156
  695.2 2.3 fusion.609
  697.5 3.6 fusion.13
  701.0 2.1 copy.576
  712.0 12.8 %all-gather.15 = bf16[8,4,2560]{2,1,0:T(4,128)(2,1)S(1)} all-gather(bf16[1,4,2560]{2,1,0:T(4,128)(2,1)S(1)} %fusion.14), channel_id=9, replica_groups=mesh['seq'=32,'tp'=8] {'tp'}, dimensions={0}, use_global_device_ids=true | all-gather | bytes 184320 | tf_op jit(solution)/shard_map/all_gather | solution.py:156
  725.6 2.3 fusion.605
  727.9 2.9 fusion.15
  738.8 17.2 %reduce-scatter.37.cloned.1.call-done = bf16[320,4]{1,0:T(8,128)(2,1)} async-done(((bf16[2560,4]{1,0:T(8,128)(2,1)}), bf16[320,4]{1,0:T(8,128)(2,1)}) %reduce-scatter.37.cloned.1.call-update) | async-done | bytes 2576
  757.8 33.7 %reduce-scatter.39.cloned.1.call-done = bf16[320,4]{1,0:T(8,128)(2,1)} async-done(((bf16[2560,4]{1,0:T(8,128)(2,1)}), bf16[320,4]{1,0:T(8,128)(2,1)}) %reduce-scatter.39.cloned.1.call-update) | async-done | bytes 2576
  (537 shorter events, 163.0 us)
Async XLA Ops:
  6.5 497.9 %copy-start = (bf16[432,2560]{1,0:T(8,128)(2,1)S(1)}, bf16[432,2560]{1,0:T(8,128)(2,1)}, u32[]{:S(2)}) copy-start(bf16[432,2560]{1,0:T(8,128)(2,1)} %param.25) | copy-start | bytes 6635524
  6.5 726.3 %reduce-scatter.25.cloned.1.call-start = ((), (), s32[]{:S(2)}) async-start(), calls=%async_computation.8 | async-start | bytes 737280
  69.5 21.6 %copy-start.8 = (bf16[1,4,2560]{2,1,0:T(4,128)(2,1)}, bf16[1,4,2560]{2,1,0:T(4,128)(2,1)S(1)}, u32[]{:S(2)}) copy-start(bf16[1,4,2560]{2,1,0:T(4,128)(2,1)S(1)} %copy.505) | copy-start | bytes 61444
  114.9 21.6 %copy-start.5 = (bf16[1,4,2560]{2,1,0:T(4,128)(2,1)}, bf16[1,4,2560]{2,1,0:T(4,128)(2,1)S(1)}, u32[]{:S(2)}) copy-start(bf16[1,4,2560]{2,1,0:T(4,128)(2,1)S(1)} %copy.528) | copy-start | bytes 61444
  165.3 21.4 %copy-start.1 = (bf16[128,1,80]{0,2,1:T(8,128)(2,1)S(1)}, bf16[128,1,80]{0,2,1:T(8,128)(2,1)}, u32[]{:S(2)}) copy-start(bf16[128,1,80]{0,2,1:T(8,128)(2,1)} %param.26) | copy-start | bytes 61444
  182.2 14.8 %copy-start.80 = (bf16[3,4,80]{2,0,1:T(4,128)(2,1)S(1)}, bf16[3,4,80]{2,0,1:T(4,128)(2,1)}, u32[]{:S(2)}) copy-start(bf16[3,4,80]{2,0,1:T(4,128)(2,1)} %fusion.260) | copy-start | bytes 5764
  182.2 15.2 %copy-start.81 = (bf16[3,4,80]{2,0,1:T(4,128)(2,1)S(1)}, bf16[3,4,80]{2,0,1:T(4,128)(2,1)}, u32[]{:S(2)}) copy-start(bf16[3,4,80]{2,0,1:T(4,128)(2,1)} %fusion.259) | copy-start | bytes 5764
  182.2 15.4 %copy-start.83 = (bf16[3,4,80]{2,0,1:T(4,128)(2,1)S(1)}, bf16[3,4,80]{2,0,1:T(4,128)(2,1)}, u32[]{:S(2)}) copy-start(bf16[3,4,80]{2,0,1:T(4,128)(2,1)} %fusion.258) | copy-start | bytes 5764
  182.2 15.6 %copy-start.82 = (bf16[3,4,80]{2,0,1:T(4,128)(2,1)S(1)}, bf16[3,4,80]{2,0,1:T(4,128)(2,1)}, u32[]{:S(2)}) copy-start(bf16[3,4,80]{2,0,1:T(4,128)(2,1)} %fusion.257) | copy-start | bytes 5764
  182.2 15.8 %copy-start.85 = (bf16[3,4,80]{2,0,1:T(4,128)(2,1)S(1)}, bf16[3,4,80]{2,0,1:T(4,128)(2,1)}, u32[]{:S(2)}) copy-start(bf16[3,4,80]{2,0,1:T(4,128)(2,1)} %fusion.256) | copy-start | bytes 5764
  182.2 16.0 %copy-start.84 = (bf16[3,4,80]{2,0,1:T(4,128)(2,1)S(1)}, bf16[3,4,80]{2,0,1:T(4,128)(2,1)}, u32[]{:S(2)}) copy-start(bf16[3,4,80]{2,0,1:T(4,128)(2,1)} %fusion.255) | copy-start | bytes 5764
  182.2 18.8 %copy-start.12 = (bf16[1,4,2560]{2,1,0:T(4,128)(2,1)S(1)}, bf16[1,4,2560]{2,1,0:T(4,128)(2,1)}, u32[]{:S(2)}) copy-start(bf16[1,4,2560]{2,1,0:T(4,128)(2,1)} %copy-done.11) | copy-start | bytes 61444
  182.2 18.8 %copy-start.94 = (f32[4]{0:T(128)S(1)}, f32[4]{0:T(128)}, u32[]{:S(2)}) copy-start(f32[4]{0:T(128)} %copy-done.93) | copy-start | bytes 52
  182.2 18.8 %copy-start.105 = (bf16[2560,80]{0,1:T(8,128)(2,1)S(1)}, bf16[2560,80]{0,1:T(8,128)(2,1)}, u32[]{:S(2)}) copy-start(bf16[2560,80]{0,1:T(8,128)(2,1)} %param.20) | copy-start | bytes 1228804
  182.3 19.1 %copy-start.14 = (bf16[1,4,2560]{2,1,0:T(4,128)(2,1)S(1)}, bf16[1,4,2560]{2,1,0:T(4,128)(2,1)}, u32[]{:S(2)}) copy-start(bf16[1,4,2560]{2,1,0:T(4,128)(2,1)} %copy.471) | copy-start | bytes 61444
  182.3 19.0 %copy-start.97 = (f32[4]{0:T(128)S(1)}, f32[4]{0:T(128)}, u32[]{:S(2)}) copy-start(f32[4]{0:T(128)} %copy-done.96) | copy-start | bytes 52
  183.2 18.4 %copy-start.44 = (bf16[1,4,1,4,40]{4,1,3,2,0:T(4,128)(2,1)S(1)}, bf16[1,4,1,4,40]{4,1,3,2,0:T(4,128)(2,1)}, u32[]{:S(2)}) copy-start(bf16[1,4,1,4,40]{4,1,3,2,0:T(4,128)(2,1)} %copy-done.43) | copy-start | bytes 3844
  183.2 18.4 %copy-start.46 = (bf16[1,4,1,4,40]{4,1,3,2,0:T(4,128)(2,1)S(1)}, bf16[1,4,1,4,40]{4,1,3,2,0:T(4,128)(2,1)}, u32[]{:S(2)}) copy-start(bf16[1,4,1,4,40]{4,1,3,2,0:T(4,128)(2,1)} %copy-done.45) | copy-start | bytes 3844
  183.2 18.5 %copy-start.56 = (f32[40]{0:T(128)S(1)}, f32[40]{0:T(128)}, u32[]{:S(2)}) copy-start(f32[40]{0:T(128)} %multiply_power_fusion) | copy-start | bytes 484
  183.2 18.5 %copy-start.69 = (f32[4]{0:T(128)S(1)}, f32[4]{0:T(128)}, u32[]{:S(2)}) copy-start(f32[4]{0:T(128)} %copy-done.68) | copy-start | bytes 52
  183.2 18.5 %copy-start.71 = (f32[4]{0:T(128)S(1)}, f32[4]{0:T(128)}, u32[]{:S(2)}) copy-start(f32[4]{0:T(128)} %copy-done.70) | copy-start | bytes 52
  183.3 19.5 %copy-start.67 = (bf16[2560]{0:T(1024)(128)(2,1)S(1)}, bf16[2560]{0:T(1024)(128)(2,1)}, u32[]{:S(2)}) copy-start(bf16[2560]{0:T(1024)(128)(2,1)} %param.18) | copy-start | bytes 15364
  183.3 302.2 %copy-start.106 = (bf16[2560,80]{0,1:T(8,128)(2,1)S(1)}, bf16[2560,80]{0,1:T(8,128)(2,1)}, u32[]{:S(2)}) copy-start(bf16[2560,80]{0,1:T(8,128)(2,1)} %param.21) | copy-start | bytes 1228804
  186.3 300.2 %copy-start.15 = (bf16[1,4,1,4,40]{4,1,3,2,0:T(4,128)(2,1)}, bf16[1,4,1,4,40]{4,1,3,2,0:T(4,128)(2,1)S(1)}, u32[]{:S(2)}) copy-start(bf16[1,4,1,4,40]{4,1,3,2,0:T(4,128)(2,1)S(1)} %get-tuple-element.75) | copy-start | bytes 3844
  186.3 300.2 %copy-start.17 = (bf16[1,4,1,4,40]{4,1,3,2,0:T(4,128)(2,1)}, bf16[1,4,1,4,40]{4,1,3,2,0:T(4,128)(2,1)S(1)}, u32[]{:S(2)}) copy-start(bf16[1,4,1,4,40]{4,1,3,2,0:T(4,128)(2,1)S(1)} %get-tuple-element.76) | copy-start | bytes 3844
  186.3 300.2 %copy-start.19 = (bf16[1,4,1,4,40]{4,1,3,2,0:T(4,128)(2,1)}, bf16[1,4,1,4,40]{4,1,3,2,0:T(4,128)(2,1)S(1)}, u32[]{:S(2)}) copy-start(bf16[1,4,1,4,40]{4,1,3,2,0:T(4,128)(2,1)S(1)} %get-tuple-element.297) | copy-start | bytes 3844
  186.4 300.2 %copy-start.21 = (bf16[1,4,1,4,40]{4,1,3,2,0:T(4,128)(2,1)}, bf16[1,4,1,4,40]{4,1,3,2,0:T(4,128)(2,1)S(1)}, u32[]{:S(2)}) copy-start(bf16[1,4,1,4,40]{4,1,3,2,0:T(4,128)(2,1)S(1)} %get-tuple-element.298) | copy-start | bytes 3844
  202.4 284.1 %copy-start.47 = (bf16[1,4,1,40]{3,1,2,0:T(4,128)(2,1)}, bf16[1,4,1,40]{3,1,2,0:T(4,128)(2,1)S(1)}, u32[]{:S(2)}) copy-start(bf16[1,4,1,40]{3,1,2,0:T(4,128)(2,1)S(1)} %get-tuple-element.218) | copy-start | bytes 964
  202.4 284.1 %copy-start.48 = (bf16[1,4,1,40]{3,1,2,0:T(4,128)(2,1)}, bf16[1,4,1,40]{3,1,2,0:T(4,128)(2,1)S(1)}, u32[]{:S(2)}) copy-start(bf16[1,4,1,40]{3,1,2,0:T(4,128)(2,1)S(1)} %get-tuple-element.219) | copy-start | bytes 964
  343.6 142.9 %copy-start.60 = (f32[1,4,1,4]{3,1,2,0:T(4,128)}, f32[1,4,1,4]{3,1,2,0:T(4,128)S(1)}, u32[]{:S(2)}) copy-start(f32[1,4,1,4]{3,1,2,0:T(4,128)S(1)} %get-tuple-element.35) | copy-start | bytes 196
  343.6 142.9 %copy-start.61 = (f32[1,4,1,4]{3,1,2,0:T(4,128)}, f32[1,4,1,4]{3,1,2,0:T(4,128)S(1)}, u32[]{:S(2)}) copy-start(f32[1,4,1,4]{3,1,2,0:T(4,128)S(1)} %get-tuple-element.34) | copy-start | bytes 196
  343.6 142.9 %copy-start.62 = (f32[1,4,1,4]{3,1,2,0:T(4,128)}, f32[1,4,1,4]{3,1,2,0:T(4,128)S(1)}, u32[]{:S(2)}) copy-start(f32[1,4,1,4]{3,1,2,0:T(4,128)S(1)} %get-tuple-element.33) | copy-start | bytes 196
  343.6 142.9 %copy-start.66 = (f32[1,4,1,4]{3,1,2,0:T(4,128)}, f32[1,4,1,4]{3,1,2,0:T(4,128)S(1)}, u32[]{:S(2)}) copy-start(f32[1,4,1,4]{3,1,2,0:T(4,128)S(1)} %get-tuple-element.30) | copy-start | bytes 196
  343.6 144.7 %copy-start.59 = (f32[1,4,1,4]{3,1,2,0:T(4,128)}, f32[1,4,1,4]{3,1,2,0:T(4,128)S(1)}, u32[]{:S(2)}) copy-start(f32[1,4,1,4]{3,1,2,0:T(4,128)S(1)} %get-tuple-element.36) | copy-start | bytes 196
  511.0 21.7 %copy-start.13 = (bf16[1,4,2560]{2,1,0:T(4,128)(2,1)S(1)}, bf16[1,4,2560]{2,1,0:T(4,128)(2,1)}, u32[]{:S(2)}) copy-start(bf16[1,4,2560]{2,1,0:T(4,128)(2,1)} %copy-done.11) | copy-start | bytes 61444
  511.1 222.8 %reduce-scatter.27.cloned.1.call-start = ((), (), s32[]{:S(2)}) async-start(), calls=%async_computation.9 | async-start | bytes 737280
  542.5 24.1 %copy-start.10 = (bf16[1,4,2560]{2,1,0:T(4,128)(2,1)S(1)}, bf16[1,4,2560]{2,1,0:T(4,128)(2,1)}, u32[]{:S(2)}) copy-start(bf16[1,4,2560]{2,1,0:T(4,128)(2,1)} %copy.492) | copy-start | bytes 61444
  542.5 192.3 %reduce-scatter.29.cloned.1.call-start = ((), (), s32[]{:S(2)}) async-start(), calls=%async_computation.10 | async-start | bytes 737280
  576.3 20.1 %copy-start.9 = (bf16[1,4,2560]{2,1,0:T(4,128)(2,1)S(1)}, bf16[1,4,2560]{2,1,0:T(4,128)(2,1)}, u32[]{:S(2)}) copy-start(bf16[1,4,2560]{2,1,0:T(4,128)(2,1)} %copy-done.8) | copy-start | bytes 61444
  576.4 159.5 %reduce-scatter.31.cloned.1.call-start = ((), (), s32[]{:S(2)}) async-start(), calls=%async_computation.11 | async-start | bytes 737280
  606.1 22.8 %copy-start.7 = (bf16[1,4,2560]{2,1,0:T(4,128)(2,1)S(1)}, bf16[1,4,2560]{2,1,0:T(4,128)(2,1)}, u32[]{:S(2)}) copy-start(bf16[1,4,2560]{2,1,0:T(4,128)(2,1)} %copy.517) | copy-start | bytes 61444
  606.1 130.7 %reduce-scatter.33.cloned.1.call-start = ((), (), s32[]{:S(2)}) async-start(), calls=%async_computation.12 | async-start | bytes 737280
  638.7 25.3 %copy-start.6 = (bf16[1,4,2560]{2,1,0:T(4,128)(2,1)S(1)}, bf16[1,4,2560]{2,1,0:T(4,128)(2,1)}, u32[]{:S(2)}) copy-start(bf16[1,4,2560]{2,1,0:T(4,128)(2,1)} %copy-done.5) | copy-start | bytes 61444
  638.7 99.2 %reduce-scatter.35.cloned.1.call-start = ((), (), s32[]{:S(2)}) async-start(), calls=%async_computation.13 | async-start | bytes 737280
  673.7 20.8 %copy-start.4 = (bf16[1,4,2560]{2,1,0:T(4,128)(2,1)S(1)}, bf16[1,4,2560]{2,1,0:T(4,128)(2,1)}, u32[]{:S(2)}) copy-start(bf16[1,4,2560]{2,1,0:T(4,128)(2,1)} %copy.539) | copy-start | bytes 61444
  673.7 82.3 %reduce-scatter.37.cloned.1.call-start = ((), (), s32[]{:S(2)}) async-start(), calls=%async_computation.14 | async-start | bytes 737280
  704.1 20.7 %copy-start.3 = (bf16[1,4,2560]{2,1,0:T(4,128)(2,1)S(1)}, bf16[1,4,2560]{2,1,0:T(4,128)(2,1)}, u32[]{:S(2)}) copy-start(bf16[1,4,2560]{2,1,0:T(4,128)(2,1)} %copy-done.2) | copy-start | bytes 61444
  704.1 87.3 %reduce-scatter.39.cloned.1.call-start = ((), (), s32[]{:S(2)}) async-start(), calls=%async_computation.15 | async-start | bytes 737280
  (70 other events, 391.9 us)
Sparse Core Ops, SparseCore 0:
  511.2 31.5 reduce-scatter.24
  545.3 32.8 reduce-scatter.26
  580.7 32.8 reduce-scatter.28
  616.0 33.0 reduce-scatter.30
  651.5 33.2 reduce-scatter.32
  687.2 32.9 reduce-scatter.34
  722.7 33.2 reduce-scatter.36
  758.5 32.8 reduce-scatter.38
